TPU v7x, 32 devices: a whole 2x2x4 slice. The times are simulated.
32 devices in a mesh: tok: 4 (over y, x), hid: 8 (over z, core).
Axes of the slice: x: 2, y: 2, z: 4, core: 2. Of those that a mesh axis runs over, the one named last changes fastest.
Arguments:
- activations: bfloat16 [4096, 4096], P('tok', 'hid'), may hold values from -6 to 6
- gate_weight: bfloat16 [4096, 14336], P(None, 'hid'), may hold values from -0.09375 to 0.09375
- up_weight: bfloat16 [4096, 14336], P(None, 'hid'), may hold values from -0.09375 to 0.09375
- row_signs: int32 [4096], P('tok'), may hold values from 0 to 1
- row_scales: float32 [4096], P('tok'), may hold values from 0.25 to 4
- kept_rows: int32 [256], P('tok'), may hold values from 0 to 1023, as said below
Outputs:
- gram_matrix: float32 [256, 256], P('tok')
Inputs may be any that keep to these rules, and one draw needn't show every extreme that they name: `kept_rows`: within each aligned block of 64 entries the values are distinct.
All inputs are finite; a program needn't handle non-finite values.
Results may differ from a plain program's by a relative error of at most 0.0014.
Values may be sent and summed in bfloat16 or wider, within the bound.
No kernel may reach another device: no remote copies, remote signals or barrier semaphores. Data moves between devices by JAX's collectives and lax.ppermute only.
A program may use at most 128 MiB of HBM per device.

v0:
```python
import jax
import jax.numpy as jnp
from jax import lax
from jax.sharding import PartitionSpec as P

FF = 14336


def bit_parity(values):
    parity = jnp.zeros_like(values)
    for shift_count in range(16):
        parity = parity ^ values >> shift_count & 1
    return parity


def hadamard_signs(first_rows, columns):
    parity = bit_parity(first_rows[:, None] & columns[None, :])
    return 1 - 2 * parity


def per_device(activations, gate_weight, up_weight, row_signs, row_scales, kept_rows):
    tok_rows = activations.shape[0]
    kept_count = kept_rows.shape[0]
    shard_count = lax.axis_size("tok")
    position = lax.axis_index("tok")
    row_scale = float(tok_rows * shard_count) ** (-0.5)
    shard_cols = lax.all_gather(activations, "hid", axis=1, tiled=True)
    gate_proj = jnp.dot(shard_cols, gate_weight, preferred_element_type=jnp.float32)
    up_proj = jnp.dot(shard_cols, up_weight, preferred_element_type=jnp.float32)
    row_factor = (2 * row_signs - 1).astype(jnp.float32) * row_scales
    signed_hidden = (row_factor[:, None] * jax.nn.silu(gate_proj) * up_proj).astype(jnp.bfloat16)
    local_positions = jnp.arange(tok_rows, dtype=jnp.int32)
    every_kept = lax.all_gather(kept_rows, "tok", axis=0, tiled=True)
    owners = jnp.arange(kept_count * lax.axis_size("tok"), dtype=jnp.int32) // kept_count
    signs_table = hadamard_signs(every_kept, local_positions).astype(jnp.bfloat16)
    partial_rows = jnp.dot(signs_table, signed_hidden, preferred_element_type=jnp.float32)
    owner_parity = bit_parity(owners & position)
    owner_sign = (1 - 2 * owner_parity).astype(jnp.float32)
    kept_values = lax.psum_scatter(
        partial_rows * owner_sign[:, None], "tok", scatter_dimension=0, tiled=True
    )
    sketch = (kept_values * row_scale).astype(jnp.bfloat16)
    gram_part = lax.dot_general(
        sketch,
        lax.all_gather(sketch, "tok", axis=0, tiled=True),
        (((1,), (1,)), ((), ())),
        preferred_element_type=jnp.float32,
    )
    gram_matrix = lax.psum(gram_part * float(FF) ** (-0.5), "hid")
    return gram_matrix


def solution(mesh):
    placed = (P("tok", "hid"), P(None, "hid"), P(None, "hid"), P("tok"), P("tok"), P("tok"))
    return jax.shard_map(
        per_device, mesh=mesh, in_specs=placed, out_specs=P("tok", None), check_vma=False
    )
```

profile of v0, /device:TPU:0, one launch (start us, length us, event | category | flops | bytes accessed | tf_op | source)
XLA Modules:
  0.0 252.6 jit_solution(3385582037482512071)
XLA Ops:
  6.5 0.0 all-gather.2.cloned.1.call-start
  6.5 0.7 all-gather.2.cloned.1.call-update
  7.3 0.0 reduce-scatter.2.cloned.1.call-start
  7.3 1.2 dynamic-slice
  9.2 0.9 dynamic-update-slice
  10.1 8.8 %all-reduce = s32[256]{0:T(256)S(1)} all-reduce(s32[256]{0:T(256)S(1)} %dynamic-update-slice), channel_id=1, replica_groups=mesh['tok'=4,'hid'=8] {'tok'}, use_global_device_ids=true, to_apply=%add | all-reduce | flops 256 | bytes 2048
  18.9 0.7 convert_multiply_fusion
  19.7 74.1 %all-gather.2.cloned.1.call-done = bf16[1024,4096]{1,0:T(8,128)(2,1)} async-done(((bf16[1024,512]{1,0:T(8,128)(2,1)}), bf16[1024,4096]{1,0:T(8,128)(2,1)}) %all-gather.2.cloned.1.call-update) | async-done | bytes 8388624 | tf_op jit(solution)/shard_map/all_gather | solution.py:27
  93.7 21.6 %fusion.35 = f32[1024,1792]{1,0:T(8,128)} fusion(bf16[1024,4096]{1,0:T(8,128)(2,1)} %all-gather.2.cloned.1.call-done, bf16[4096,1792]{1,0:T(8,128)(2,1)} %param.7), kind=kOutput, calls=%fused_computation.46 | convolution fusion | flops 15032385536 | bytes 30408704 | tf_op jit(solution)/shard_map/dot_general | solution.py:28
  115.4 28.6 %convolution_multiply_fusion = f32[256,1792]{1,0:T(8,128)} fusion(f32[1024,1792]{1,0:T(8,128)} %fusion.35, bf16[1024,4096]{1,0:T(8,128)(2,1)} %all-gather.2.cloned.1.call-done, bf16[4096,1792]{1,0:T(8,128)(2,1)} %param.8, f32[1024]{0:T(1024)S(1)} %convert_multiply_fusion, f32[256]{0:T(256)S(1)} %subtract_convert_fusion.2, s32[256]{0:T(256)S(1)} %all-reduce), kind=kOutput, calls=%fused_computation.1 | convolution fusion | flops 15998582784 | bytes 32249856 | tf_op jit(solution)/shard_map/dot_general | solution.py:36
  144.0 0.0 reduce-scatter.2.cloned.1.call-update
  144.0 0.0 all-reduce.3.cloned.1.call-start
  144.1 31.6 %reduce-scatter.2.cloned.1.call-done = f32[64,1792]{1,0:T(8,128)} async-done(((f32[256,1792]{1,0:T(8,128)}), f32[64,1792]{1,0:T(8,128)}) %reduce-scatter.2.cloned.1.call-update) | async-done | bytes 458768 | tf_op jit(solution)/shard_map/reduce_scatter | solution.py:39
  175.7 1.0 multiply_convert_fusion.1
  176.7 11.9 %all_gather.11 = bf16[256,1792]{1,0:T(8,128)(2,1)S(1)} all-gather(bf16[64,1792]{1,0:T(8,128)(2,1)S(1)} %multiply_convert_fusion.1), channel_id=1, replica_groups=mesh['tok'=4,'hid'=8] {'tok'}, dimensions={0}, use_global_device_ids=true | all-gather | bytes 1146880 | tf_op jit(solution)/shard_map/all_gather | solution.py:45
  188.6 1.1 convolution_multiply_fusion.1
  189.7 0.0 all-reduce.3.cloned.1.call-update
  189.7 54.9 %all-reduce.3.cloned.1.call-done = f32[64,256]{1,0:T(8,128)} async-done(((f32[64,256]{1,0:T(8,128)}), f32[64,256]{1,0:T(8,128)}) %all-reduce.3.cloned.1.call-update) | async-done | bytes 65552 | tf_op jit(solution)/shard_map/psum | solution.py:49
  244.6 1.5 copy.9
  (2 shorter events, 0.0 us)
Async XLA Ops:
  6.5 87.2 %all-gather.2.cloned.1.call-start = ((), (), s32[]{:S(2)}) async-start(), calls=%async_computation.1 | async-start | bytes 9437184 | tf_op jit(solution)/shard_map/all_gather | solution.py:27
  7.3 168.4 %reduce-scatter.2.cloned.1.call-start = ((), (), s32[]{:S(2)}) async-start(), calls=%async_computation.2 | async-start | bytes 2293760 | tf_op jit(solution)/shard_map/reduce_scatter | solution.py:39
  144.0 100.5 %all-reduce.3.cloned.1.call-start = ((), (), s32[]{:S(2)}) async-start(), calls=%async_computation.3 | async-start | bytes 131072 | tf_op jit(solution)/shard_map/psum | solution.py:49
Sparse Core Ops, SparseCore 0:
  8.9 84.7 all-gather.1
  144.2 31.4 reduce-scatter.1
  189.8 54.6 all-reduce.2
where the time goes:
time: 253 us
  waiting for transfers between devices  161 us (64%)
  matrix products  51.3 us (20%)
  blocking collectives  20.7 us (8%)
  between operations  13.8 us (5%)
  local copies, waits for them, and re-layouts  3.57 us (1%)
    all_gather x1, waiting for transfers between devices, per_device(): shard_cols = lax.all_gather(activations, 'hid', axis=1, tiled=True)  74.1 us
    psum x1, waiting for transfers between devices, per_device(): gram_matrix = lax.psum(gram_part * float(FF) ** (-0.5), 'hid')  54.9 us
    reduce_scatter x1, waiting for transfers between devices, per_device(): lax.psum_scatter(partial_rows * owner_sign[:, None], 'tok', scatter_dimen...  31.6 us
    dot_general x1, matrix products, per_device(): jnp.dot(signs_table, signed_hidden, preferred_element_type=jnp.float32)  28.6 us
    dot_general x1, matrix products, per_device(): jnp.dot(shard_cols, gate_weight, preferred_element_type=jnp.float32)  21.6 us
    all_gather x1, blocking collectives, per_device(): lax.all_gather(sketch, 'tok', axis=0, tiled=True)  11.9 us
    unnamed x1, blocking collectives  8.85 us
  transfers between devices with their start and end apart: 3, of which 3 were waited for; matrix products, arithmetic and copies ran while one was open for 1% of the time, Pallas kernels for 0%

commit v1 on v0

v1 whole, which is shorter than its diff:
```python
import functools

import jax
import jax.numpy as jnp
from jax import lax
from jax.experimental import pallas as pl
from jax.experimental.pallas import tpu as pltpu
from jax.sharding import PartitionSpec as P

F32, BF16 = jnp.float32, jnp.bfloat16
VMEM = pl.BlockSpec(memory_space=pltpu.VMEM)
SMEM = pl.BlockSpec(memory_space=pltpu.SMEM)
HBM = pl.BlockSpec(memory_space=pltpu.HBM)


def parity_signs(rows, columns):
    bits = rows[:, None] & columns[None, :]
    for shift in (16, 8, 4, 2, 1):
        bits = bits ^ (bits >> shift)
    return 1 - 2 * (bits & 1)


def column_tile(columns):
    for tile in (896, 512, 256, 128):
        if columns % tile == 0:
            return tile
    return columns


def weight_copies(index, gate, up, buffer, sem, depth, tile, step, slot):
    columns = pl.ds(pl.multiple_of(step * tile, tile), tile)
    return [
        pltpu.make_async_copy(
            weight.at[pl.ds(pl.multiple_of(index[half] * depth, depth), depth), columns],
            buffer.at[slot, which, pl.ds(half * depth, depth)],
            sem.at[slot, which, half],
        )
        for which, weight in enumerate((gate, up))
        for half in range(2)
    ]


def over_tiles(index, gate, up, buffer, sem, depth, tile, count, work):
    args = (index, gate, up, buffer, sem, depth, tile)
    for copy in weight_copies(*args, 0, 0):
        copy.start()

    def step(tile_index, carry):
        slot = lax.rem(tile_index, 2)

        @pl.when(tile_index + 1 < count)
        def _():
            for copy in weight_copies(*args, tile_index + 1, 1 - slot):
                copy.start()

        for copy in weight_copies(*args, tile_index, slot):
            copy.wait()
        work(slot, pl.ds(pl.multiple_of(tile_index * tile, tile), tile))
        return carry

    lax.fori_loop(0, count, step, 0)


def product(near, far, buffer, slot, which, depth):
    return jnp.dot(
        near[...], buffer[slot, which, :depth], preferred_element_type=F32
    ) + jnp.dot(far[...], buffer[slot, which, depth:], preferred_element_type=F32)


def first_kernel(tile, index, near, far, gate, up, total, buffer, sem):
    depth = near.shape[1]

    def work(slot, columns):
        for which in range(2):
            total[which, :, columns] = product(near, far, buffer, slot, which, depth)

    over_tiles(index, gate, up, buffer, sem, depth, tile, total.shape[2] // tile, work)


def more_kernel(tile, index, near, far, before, gate, up, total, buffer, sem):
    depth = near.shape[1]

    def work(slot, columns):
        for which in range(2):
            total[which, :, columns] = before[which, :, columns] + product(
                near, far, buffer, slot, which, depth
            )

    over_tiles(index, gate, up, buffer, sem, depth, tile, total.shape[2] // tile, work)


def accumulate(index, near, far, gate, up, before=None):
    rows, depth = near.shape
    columns = gate.shape[1]
    tile = column_tile(columns)
    kernel = first_kernel if before is None else more_kernel
    held = [] if before is None else [before]
    return pl.pallas_call(
        functools.partial(kernel, tile),
        out_shape=jax.ShapeDtypeStruct((2, rows, columns), F32),
        in_specs=[SMEM, VMEM, VMEM] + [VMEM] * len(held) + [HBM, HBM],
        out_specs=VMEM,
        scratch_shapes=[
            pltpu.VMEM((2, 2, 2 * depth, tile), BF16),
            pltpu.SemaphoreType.DMA((2, 2, 2)),
        ],
        input_output_aliases={3: 0} if held else {},
        compiler_params=pltpu.CompilerParams(vmem_limit_bytes=24 << 20),
        cost_estimate=pl.CostEstimate(
            flops=8 * rows * depth * columns, bytes_accessed=8 * depth * columns, transcendentals=0
        ),
    )(index, near, far, *held, gate, up)


def finish_kernel(tile, offset, held, index, near, far, before, factor, signs, *refs):
    depth = near.shape[1]
    rows = near.shape[0]
    if held:
        part_in, gate, up, part, buffer, sem = refs
    else:
        gate, up, part, buffer, sem = refs

    def work(slot, columns):
        span = pl.ds(offset, rows)
        gate_proj = before[0, span, columns] + product(near, far, buffer, slot, 0, depth)
        up_proj = before[1, span, columns] + product(near, far, buffer, slot, 1, depth)
        hidden = factor[...] * (gate_proj / (1 + jnp.exp(-gate_proj))) * up_proj
        rows_part = jnp.dot(signs[...], hidden.astype(BF16), preferred_element_type=F32)
        part[:, columns] = rows_part + part_in[:, columns] if held else rows_part

    over_tiles(index, gate, up, buffer, sem, depth, tile, before.shape[2] // tile, work)


def finish(index, near, far, before, offset, factor, signs, gate, up, part=None):
    rows, depth = near.shape
    columns = gate.shape[1]
    kept = signs.shape[0]
    tile = 256 if columns % 256 == 0 else columns
    held = [] if part is None else [part]
    return pl.pallas_call(
        functools.partial(finish_kernel, tile, offset, bool(held)),
        out_shape=jax.ShapeDtypeStruct((kept, columns), F32),
        in_specs=[SMEM] + [VMEM] * (5 + len(held)) + [HBM, HBM],
        out_specs=VMEM,
        scratch_shapes=[
            pltpu.VMEM((2, 2, 2 * depth, tile), BF16),
            pltpu.SemaphoreType.DMA((2, 2, 2)),
        ],
        input_output_aliases={6: 0} if held else {},
        compiler_params=pltpu.CompilerParams(vmem_limit_bytes=24 << 20),
        cost_estimate=pl.CostEstimate(
            flops=8 * rows * depth * columns + 2 * kept * rows * columns,
            bytes_accessed=8 * depth * columns,
            transcendentals=rows * columns,
        ),
    )(index, near, far, before, factor, signs, *held, gate, up)


def swap_pairs(count, mask):
    return [(place, place ^ mask) for place in range(count)]


def line_pairs(pairs, parity, step):
    moves = []
    for place in range(pairs):
        upward = place % 2 == parity
        other = place + 1 if upward else place - 1
        block = place + step if upward else place - step
        if 0 <= other < pairs and 0 <= block < pairs:
            moves += [(2 * other + core, 2 * place + core) for core in range(2)]
    return moves


def tokens_exchanged(values, shards, position):
    rows = values.shape[0] // shards

    def block(mask):
        return lax.dynamic_slice_in_dim(values, (position ^ mask) * rows, rows, 0)

    moved = [
        lax.ppermute(block(mask), "tok", swap_pairs(shards, mask)) for mask in range(1, shards)
    ]
    total = block(0).astype(F32)
    for piece in moved:
        total = total + piece.astype(F32)
    return total


def line_device(activations, gate_weight, up_weight, row_signs, row_scales, kept_rows):
    tok_rows, depth = activations.shape
    shards = lax.axis_size("tok")
    hid = lax.axis_size("hid")
    pairs = hid // 2
    position = lax.axis_index("tok")
    place = lax.axis_index("hid")
    line, core = place // 2, place % 2
    even = line % 2 == 0
    half = tok_rows // 2

    def over_hid(values, moves):
        return lax.ppermute(values, "hid", moves)

    def twin(values):
        return over_hid(values, swap_pairs(hid, 1))

    every = [kept_rows] + [
        lax.ppermute(kept_rows, "tok", swap_pairs(shards, mask)) for mask in range(1, shards)
    ]
    every = jnp.stack(every)[jnp.arange(shards) ^ position]
    kept = kept_rows.shape[0] * shards
    every = (every + tok_rows * jnp.arange(shards, dtype=jnp.int32)[:, None]).reshape(kept)
    local = position * tok_rows + jnp.arange(tok_rows, dtype=jnp.int32)
    signs = parity_signs(every, local).astype(BF16)
    factor = ((2 * row_signs - 1).astype(F32) * row_scales)[:, None]

    halves = [activations[:half], activations[half:]]
    even_got = {1: [over_hid(part, line_pairs(pairs, 0, 1)) for part in halves]}
    odd_got = {1: [over_hid(part, line_pairs(pairs, 1, 1)) for part in halves]}
    blocks = [line]
    arrived = [even_got[1]]
    toward = jnp.where(even, 1, -1)
    blocks.append(line + toward)
    for step in range(2, pairs):
        even_got[step] = [over_hid(part, line_pairs(pairs, 0, step)) for part in odd_got[step - 1]]
        if step < pairs - 1:
            odd_got[step] = [
                over_hid(part, line_pairs(pairs, 1, step)) for part in even_got[step - 1]
            ]
        ahead = line + toward * step
        valid = (ahead >= 0) & (ahead < pairs)
        arrived.append(
            [jnp.where(valid, e, o) for e, o in zip(even_got[step], odd_got[step - 1])]
        )
        blocks.append(jnp.where(valid, ahead, line - toward * (step - 1)))

    def index_of(block):
        return jnp.stack([2 * block + core, 2 * block + 1 - core]).astype(jnp.int32)

    weights = (gate_weight, up_weight)
    own_twin = twin(activations)
    totals = [
        accumulate(index_of(line), halves[s], own_twin[s * half : (s + 1) * half], *weights)
        for s in range(2)
    ]
    for step in range(pairs - 2):
        for s in range(2):
            near = arrived[step][s]
            totals[s] = accumulate(
                index_of(blocks[step + 1]), near, twin(near), *weights, totals[s]
            )
    part = None
    for s in range(2):
        near = arrived[-1][s]
        rows = slice(s * half, (s + 1) * half)
        part = finish(
            index_of(blocks[-1]), near, twin(near), totals[s], 0,
            factor[rows], signs[:, rows], *weights, part,
        )

    turned = part.T.astype(BF16)
    columns = gate_weight.shape[1]
    scale = float(tok_rows * shards) ** -0.5
    sketch = (tokens_exchanged(turned, shards, position) * scale).astype(BF16)
    gram = lax.dot_general(
        sketch, sketch, (((0,), (0,)), ((), ())), preferred_element_type=F32
    ) * (float(columns * hid) ** -0.5)
    total = tokens_exchanged(gram, shards, position)
    moved = [over_hid(total, swap_pairs(hid, 2 * mask)) for mask in range(1, pairs)]
    for piece in moved:
        total = total + piece
    return total + twin(total)


def gather_device(activations, gate_weight, up_weight, row_signs, row_scales, kept_rows):
    tok_rows = activations.shape[0]
    shards = lax.axis_size("tok")
    position = lax.axis_index("tok")
    columns = gate_weight.shape[1] * lax.axis_size("hid")
    whole = lax.all_gather(activations, "hid", axis=1, tiled=True)
    gate_proj = jnp.dot(whole, gate_weight, preferred_element_type=F32)
    up_proj = jnp.dot(whole, up_weight, preferred_element_type=F32)
    factor = (2 * row_signs - 1).astype(F32) * row_scales
    hidden = (factor[:, None] * jax.nn.silu(gate_proj) * up_proj).astype(BF16)
    every = lax.all_gather(kept_rows, "tok", axis=0, tiled=True)
    owner = jnp.arange(every.shape[0], dtype=jnp.int32) // kept_rows.shape[0]
    local = position * tok_rows + jnp.arange(tok_rows, dtype=jnp.int32)
    signs = parity_signs(owner * tok_rows + every, local).astype(BF16)
    part = jnp.dot(signs, hidden, preferred_element_type=F32)
    mine = lax.psum_scatter(part, "tok", scatter_dimension=0, tiled=True)
    sketch = (mine * float(tok_rows * shards) ** -0.5).astype(BF16)
    gram = lax.dot_general(
        sketch,
        lax.all_gather(sketch, "tok", axis=0, tiled=True),
        (((1,), (1,)), ((), ())),
        preferred_element_type=F32,
    )
    return lax.psum(gram * float(columns) ** -0.5, "hid")


def solution(mesh):
    short = mesh.shape["hid"] % 2 == 0 and 2 < mesh.shape["hid"] // 2 <= 4
    placed = (P("tok", "hid"), P(None, "hid"), P(None, "hid"), P("tok"), P("tok"), P("tok"))
    return jax.shard_map(
        line_device if short else gather_device,
        mesh=mesh,
        in_specs=placed,
        out_specs=P("tok", None),
        check_vma=False,
    )
```

time: 253 us -> 178 us (0.70)
  waiting for transfers between devices: 161 us -> 44.9 us
  Pallas kernels: 0 us -> 64.1 us
  matrix products: 51.3 us -> 0.48 us
  starting transfers between devices: 0.08 us -> 40.7 us
  blocking collectives: 20.7 us -> 0 us
  local copies, waits for them, and re-layouts: 3.57 us -> 21.7 us
  between operations: 13.8 us -> 0.45 us
  other arithmetic: 1.79 us -> 4.35 us
    all_gather x1 -> x0, waiting for transfers between devices: 74.1 us -> none  [per_device(): shard_cols = lax.all_gather(activations, 'hid', axis=1, tiled=True)]
    pallas_call x0 -> x8, Pallas kernels: none -> 64.1 us  [the longest x6 46.3 us: accumulate(): pl.pallas_call(functools.partial(kernel, tile), out_shape=jax.ShapeDtypeS...]
    psum x1 -> x0, waiting for transfers between devices: 54.9 us -> none  [per_device(): gram_matrix = lax.psum(gram_part * float(FF) ** (-0.5), 'hid')]
    dot_general x3 -> x1, matrix products: 51.3 us -> 0.48 us  [line_device(): lax.dot_general(sketch, sketch, (((0,), (0,)), ((), ())), preferred_eleme...]
    ppermute x0 -> x30, waiting for transfers between devices: none -> 44.9 us  [the longest x21 29.2 us: over_hid(): return lax.ppermute(values, 'hid', moves)]
    ppermute x0 -> x30, starting transfers between devices: none -> 40.7 us  [the longest x21 29.1 us: over_hid(): return lax.ppermute(values, 'hid', moves)]
    reduce_scatter x1 -> x0, waiting for transfers between devices: 31.6 us -> none  [per_device(): lax.psum_scatter(partial_rows * owner_sign[:, None], 'tok', scatter_dimen...]
    unnamed x4 -> x24, local copies, waits for them, and re-layouts: 3.57 us -> 17.1 us
  transfers between devices with their start and end apart: 3 -> 30, of which waited for: 3 -> 12; matrix products, arithmetic and copies ran while one was open for 1% -> 4% of each run, Pallas kernels for 0% -> 31%
where the time goes in v1:
time: 178 us; the launch traced here: 177 us
  Pallas kernels  64.1 us (36%)
  waiting for transfers between devices  44.9 us (25%)
  starting transfers between devices  40.7 us (23%)
  local copies, waits for them, and re-layouts  21.7 us (12%)
  other arithmetic  4.35 us (2%)
    pallas_call x6, Pallas kernels, accumulate(): pl.pallas_call(functools.partial(kernel, tile), out_shape=jax.ShapeDtypeS...  46.3 us
    ppermute x21, waiting for transfers between devices, over_hid(): return lax.ppermute(values, 'hid', moves)  29.2 us
    ppermute x21, starting transfers between devices, over_hid(): return lax.ppermute(values, 'hid', moves)  29.1 us
    pallas_call x2, Pallas kernels, finish(): pl.pallas_call(functools.partial(finish_kernel, tile, offset, bool(held))...  17.8 us
    unnamed x24, local copies, waits for them, and re-layouts  17.1 us
    ppermute x6, waiting for transfers between devices, tokens_exchanged(): lax.ppermute(block(mask), 'tok', swap_pairs(shards, mask))  15.8 us
    ppermute x6, starting transfers between devices, tokens_exchanged(): lax.ppermute(block(mask), 'tok', swap_pairs(shards, mask))  7.11 us
    ppermute x3, starting transfers between devices, line_device(): lax.ppermute(kept_rows, 'tok', swap_pairs(shards, mask))  4.49 us
  transfers between devices with their start and end apart: 30, of which 12 were waited for; matrix products, arithmetic and copies ran while one was open for 4% of the time, Pallas kernels for 31%

profile of v1, /device:TPU:0, one launch (start us, length us, event | category | flops | bytes accessed | tf_op | source)
XLA Modules:
  0.0 176.8 jit_solution(14996589283110838371)
XLA Ops:
  0.0 3.0 %collective-permute-start.9 = (s32[64]{0:T(128)}, s32[64]{0:T(128)S(1)}, u32[]{:S(2)}, u32[]{:S(2)}) collective-permute-start(s32[64]{0:T(128)} %param.11), channel_id=1, source_target_pairs={{0,8},{8,0},{16,24},{24,16},{1,9},{9,1},{17,25},{25,17},{2,10},{10... | collective-permute-start | bytes 776 | tf_op jit(solution)/shard_map/ppermute | solution.py:207
  3.0 1.5 collective-permute-start.10
  4.5 1.3 fusion.15
  5.8 2.1 %collective-permute-start.12 = (bf16[512,512]{1,0:T(8,128)(2,1)S(1)}, bf16[512,512]{1,0:T(8,128)(2,1)}, u32[]{:S(2)}, u32[]{:S(2)}) collective-permute-start(bf16[512,512]{1,0:T(8,128)(2,1)S(1)} %get-tuple-element.7.near), channel_id=1, source_target_pairs={{2,0},{3,1},{0,2},{1,3},{6,4},{7,5},{4,6},{5,7},{10,8},{11,9},{8,1... | collective-permute-start | bytes 1572872 | tf_op jit(solution)/shard_map/ppermute | solution.py:201
  8.8 0.9 copy.12.factor
  9.9 1.5 collective-permute-start.16
  11.4 3.7 %collective-permute-start = (bf16[512,512]{1,0:T(8,128)(2,1)S(1)}, bf16[512,512]{1,0:T(8,128)(2,1)}, u32[]{:S(2)}, u32[]{:S(2)}) collective-permute-start(bf16[512,512]{1,0:T(8,128)(2,1)S(1)} %get-tuple-element.8.near), channel_id=1, source_target_pairs={{2,0},{3,1},{0,2},{1,3},{6,4},{7,5},{4,6},{5,7},{10,8},{11,9},{8,1... | collective-permute-start | bytes 1572872 | tf_op jit(solution)/shard_map/ppermute | solution.py:201
  15.0 1.5 collective-permute-start.4
  18.6 2.2 %collective-permute-done.12.near = bf16[512,512]{1,0:T(8,128)(2,1)} collective-permute-done((bf16[512,512]{1,0:T(8,128)(2,1)S(1)}, bf16[512,512]{1,0:T(8,128)(2,1)}, u32[]{:S(2)}, u32[]{:S(2)}) %collective-permute-start.12) | collective-permute-done | bytes 524320 | tf_op jit(solution)/shard_map/ppermute | solution.py:201
  20.8 1.5 collective-permute-start.13
  22.2 9.6 %collective-permute-done.near = bf16[512,512]{1,0:T(8,128)(2,1)} collective-permute-done((bf16[512,512]{1,0:T(8,128)(2,1)S(1)}, bf16[512,512]{1,0:T(8,128)(2,1)}, u32[]{:S(2)}, u32[]{:S(2)}) %collective-permute-start) | collective-permute-done | bytes 524320 | tf_op jit(solution)/shard_map/ppermute | solution.py:201
  31.8 1.3 collective-permute-start.17
  33.2 1.3 collective-permute-start.5
  34.5 1.3 fusion.14
  35.8 5.2 %copy-done = bf16[4096,1792]{1,0:T(8,128)(2,1)S(1)} copy-done((bf16[4096,1792]{1,0:T(8,128)(2,1)S(1)}, bf16[4096,1792]{1,0:T(8,128)(2,1)}, u32[]{:S(2)}) %copy-start) | copy-done | bytes 14680088
  41.0 7.3 %shard_map.67.before = f32[2,512,1792]{2,1,0:T(8,128)S(1)} custom-call(s32[2]{0:T(128)S(1)} %pad_add_fusion.4.index, bf16[512,512]{1,0:T(8,128)(2,1)S(1)} %get-tuple-element.7.near, bf16[512,512]{1,0:T(8,128)(2,1)S(1)} %get-tuple-element.5.far, bf16[4096,1792]{1,0:T(8,128)(2,1)S(1)} %copy-done, bf16[4096,1792]{1,0:T(8,128)(2,1)} %refs_2_.1), custom_call_target="tpu_custom_call" | custom-call | flops 3758096384 | bytes 7340032 | tf_op jit(solution)/shard_map/pallas_call | solution.py:98
  48.3 8.3 %shard_map.64.before = f32[2,512,1792]{2,1,0:T(8,128)S(1)} custom-call(s32[2]{0:T(128)S(1)} %pad_add_fusion.4.index, bf16[512,512]{1,0:T(8,128)(2,1)S(1)} %get-tuple-element.8.near, bf16[512,512]{1,0:T(8,128)(2,1)S(1)} %get-tuple-element.6.far, bf16[4096,1792]{1,0:T(8,128)(2,1)S(1)} %bitcast.34, bf16[4096,1792]{1,0:T(8,128)(2,1)} %refs_2_.1), custom_call_target="tpu_custom_call" | custom-call | flops 3758096384 | bytes 7340032 | tf_op jit(solution)/shard_map/pallas_call | solution.py:98
  57.4 1.6 collective-permute-done.5
  59.0 1.1 broadcast_select_fusion.1.near
  60.7 1.3 collective-permute-start.14
  62.0 1.5 collective-permute-start.2
  63.5 3.1 %copy-done.2 = f32[2,512,1792]{2,1,0:T(8,128)S(1)} copy-done((f32[2,512,1792]{2,1,0:T(8,128)S(1)}, f32[2,512,1792]{2,1,0:T(8,128)}, u32[]{:S(2)}) %copy-start.2) | copy-done | bytes 7340056
  66.6 7.8 %shard_map.68.before = f32[2,512,1792]{2,1,0:T(8,128)S(1)} custom-call(s32[2]{0:T(128)S(1)} %pad_add_fusion.3.index, bf16[512,512]{1,0:T(8,128)(2,1)} %collective-permute-done.12.near, bf16[512,512]{1,0:T(8,128)(2,1)S(1)} %collective-permute-done.19.far, f32[2,512,1792]{2,1,0:T(8,128)S(1)} %copy-done.2, ...), custom_call_target="tpu_custom_call", output_to_operand_aliasing={{}: (3, {})} | custom-call | flops 3758096384 | bytes 7340032 | tf_op jit(solution)/shard_map/pallas_call | solution.py:98
  74.4 2.9 %copy-done.3 = f32[2,512,1792]{2,1,0:T(8,128)} copy-done((f32[2,512,1792]{2,1,0:T(8,128)}, f32[2,512,1792]{2,1,0:T(8,128)S(1)}, u32[]{:S(2)}) %copy-start.3) | copy-done | bytes 7340056
  77.3 7.8 %shard_map.65.before = f32[2,512,1792]{2,1,0:T(8,128)S(1)} custom-call(s32[2]{0:T(128)S(1)} %pad_add_fusion.3.index, bf16[512,512]{1,0:T(8,128)(2,1)} %collective-permute-done.near, bf16[512,512]{1,0:T(8,128)(2,1)S(1)} %collective-permute-done.7.far, f32[2,512,1792]{2,1,0:T(8,128)S(1)} %shard_map.64.before, ...), custom_call_target="tpu_custom_call", output_to_operand_aliasing={{}: (3, {})} | custom-call | flops 3758096384 | bytes 7340032 | tf_op jit(solution)/shard_map/pallas_call | solution.py:98
  85.4 9.8 %collective-permute-done.2 = bf16[512,512]{1,0:T(8,128)(2,1)S(1)} collective-permute-done((bf16[512,512]{1,0:T(8,128)(2,1)S(1)}, bf16[512,512]{1,0:T(8,128)(2,1)S(1)}, u32[]{:S(2)}, u32[]{:S(2)}) %collective-permute-start.2) | collective-permute-done | bytes 524320 | tf_op jit(solution)/shard_map/ppermute | solution.py:201
  95.3 3.1 %copy-done.4 = f32[2,512,1792]{2,1,0:T(8,128)S(1)} copy-done((f32[2,512,1792]{2,1,0:T(8,128)S(1)}, f32[2,512,1792]{2,1,0:T(8,128)}, u32[]{:S(2)}) %copy-start.4) | copy-done | bytes 7340056
  98.4 7.3 %shard_map.69.before = f32[2,512,1792]{2,1,0:T(8,128)S(1)} custom-call(s32[2]{0:T(128)S(1)} %get-tuple-element.20.index, bf16[512,512]{1,0:T(8,128)(2,1)S(1)} %broadcast_select_fusion.near, bf16[512,512]{1,0:T(8,128)(2,1)S(1)} %collective-permute-done.18.far, f32[2,512,1792]{2,1,0:T(8,128)S(1)} %copy-done.4, ...), custom_call_target="tpu_custom_call", output_to_operand_aliasing={{}: (3, {})} | custom-call | flops 3758096384 | bytes 7340032 | tf_op jit(solution)/shard_map/pallas_call | solution.py:98
  105.7 2.9 %copy-done.5 = f32[2,512,1792]{2,1,0:T(8,128)} copy-done((f32[2,512,1792]{2,1,0:T(8,128)}, f32[2,512,1792]{2,1,0:T(8,128)S(1)}, u32[]{:S(2)}) %copy-start.5) | copy-done | bytes 7340056
  108.6 7.7 %shard_map.66.before = f32[2,512,1792]{2,1,0:T(8,128)S(1)} custom-call(s32[2]{0:T(128)S(1)} %get-tuple-element.20.index, bf16[512,512]{1,0:T(8,128)(2,1)S(1)} %broadcast_select_fusion.1.near, bf16[512,512]{1,0:T(8,128)(2,1)S(1)} %collective-permute-done.6.far, f32[2,512,1792]{2,1,0:T(8,128)S(1)} %shard_map.65.before, ...), custom_call_target="tpu_custom_call", output_to_operand_aliasing={{}: (3, {})} | custom-call | flops 3758096384 | bytes 7340032 | tf_op jit(solution)/shard_map/pallas_call | solution.py:98
  116.3 8.9 %shard_map.70.refs_0_ = f32[256,1792]{1,0:T(8,128)S(1)} custom-call(s32[2]{0:T(128)S(1)} %get-tuple-element.19.index, bf16[512,512]{1,0:T(8,128)(2,1)S(1)} %broadcast_select_fusion.2.near, bf16[512,512]{1,0:T(8,128)(2,1)S(1)} %collective-permute-done.15.far, f32[2,512,1792]{2,1,0:T(8,128)S(1)} %copy-done.6, f32[512,1]{1,0:T(8,128)S(1)} %copy-done.7, ...), custom_call_target="tpu_custom_call" | custom-call | flops 4227858432 | bytes 7340032 | tf_op jit(solution)/shard_map/pallas_call | solution.py:140
  125.2 8.9 %shard_map.71 = f32[256,1792]{1,0:T(8,128)S(1)} custom-call(s32[2]{0:T(128)S(1)} %get-tuple-element.19.index, bf16[512,512]{1,0:T(8,128)(2,1)S(1)} %broadcast_select_fusion.3.near, bf16[512,512]{1,0:T(8,128)(2,1)S(1)} %collective-permute-done.3.far, f32[2,512,1792]{2,1,0:T(8,128)S(1)} %shard_map.66.before, ...), custom_call_target="tpu_custom_call", output_to_operand_aliasing={{}: (6, {})} | custom-call | flops 4227858432 | bytes 7340032 | tf_op jit(solution)/shard_map/pallas_call | solution.py:140
  134.6 1.6 collective-permute-start.20
  136.1 1.5 collective-permute-start.21
  138.1 5.7 %collective-permute-done.20 = bf16[448,256]{0,1:T(8,128)(2,1)S(1)} collective-permute-done((bf16[448,256]{0,1:T(8,128)(2,1)S(1)}, bf16[448,256]{0,1:T(8,128)(2,1)S(1)}, u32[]{:S(2)}, u32[]{:S(2)}) %collective-permute-start.20) | collective-permute-done | bytes 229408 | tf_op jit(solution)/shard_map/ppermute | solution.py:181
  143.8 6.3 %collective-permute-done.21 = bf16[448,256]{0,1:T(8,128)(2,1)S(1)} collective-permute-done((bf16[448,256]{0,1:T(8,128)(2,1)S(1)}, bf16[448,256]{0,1:T(8,128)(2,1)S(1)}, u32[]{:S(2)}, u32[]{:S(2)}) %collective-permute-start.21) | collective-permute-done | bytes 229408 | tf_op jit(solution)/shard_map/ppermute | solution.py:181
  150.7 1.3 collective-permute-start.23
  152.0 0.8 collective-permute-start.24
  152.8 1.4 collective-permute-start.25
  154.2 0.8 collective-permute-done.23
  155.0 1.6 collective-permute-done.24
  156.6 1.3 collective-permute-done.25
  158.0 9.4 %collective-permute-start.26 = (f32[64,256]{1,0:T(8,128)S(1)}, f32[64,256]{1,0:T(8,128)S(1)}, u32[]{:S(2)}, u32[]{:S(2)}) collective-permute-start(f32[64,256]{1,0:T(8,128)S(1)} %add_add_fusion.1), channel_id=1, source_target_pairs={{0,2},{1,3},{2,0},{3,1},{4,6},{5,7},{6,4},{7,5},{8,10},{9,11},{10,... | collective-permute-start | bytes 196616 | tf_op jit(solution)/shard_map/ppermute | solution.py:201
  167.4 1.2 collective-permute-start.27
  168.6 1.4 collective-permute-start.28
  170.0 3.2 %collective-permute-done.27 = f32[64,256]{1,0:T(8,128)S(1)} collective-permute-done((f32[64,256]{1,0:T(8,128)S(1)}, f32[64,256]{1,0:T(8,128)S(1)}, u32[]{:S(2)}, u32[]{:S(2)}) %collective-permute-start.27) | collective-permute-done | bytes 65568 | tf_op jit(solution)/shard_map/ppermute | solution.py:201
  173.3 1.5 collective-permute-done.28
  174.9 1.2 collective-permute-done.29
  (75 shorter events, 7.1 us)
Async XLA Ops:
  0.0 9.9 %collective-permute-start.9 = (s32[64]{0:T(128)}, s32[64]{0:T(128)S(1)}, u32[]{:S(2)}, u32[]{:S(2)}) collective-permute-start(s32[64]{0:T(128)} %param.11), channel_id=1, source_target_pairs={{0,8},{8,0},{16,24},{24,16},{1,9},{9,1},{17,25},{25,17},{2,10},{10... | collective-permute-start | bytes 776 | tf_op jit(solution)/shard_map/ppermute | solution.py:207
  3.0 8.4 %collective-permute-start.10 = (s32[64]{0:T(128)}, s32[64]{0:T(128)S(1)}, u32[]{:S(2)}, u32[]{:S(2)}) collective-permute-start(s32[64]{0:T(128)} %param.11), channel_id=1, source_target_pairs={{0,16},{8,24},{16,0},{24,8},{1,17},{9,25},{17,1},{25,9},{2,18},{10... | collective-permute-start | bytes 776 | tf_op jit(solution)/shard_map/ppermute | solution.py:207
  4.5 10.6 %collective-permute-start.11 = (s32[64]{0:T(128)}, s32[64]{0:T(128)S(1)}, u32[]{:S(2)}, u32[]{:S(2)}) collective-permute-start(s32[64]{0:T(128)} %param.11), channel_id=1, source_target_pairs={{0,24},{8,16},{16,8},{24,0},{1,25},{9,17},{17,9},{25,1},{2,26},{10... | collective-permute-start | bytes 776 | tf_op jit(solution)/shard_map/ppermute | solution.py:207
  4.5 28.7 %collective-permute-start.8 = (bf16[1024,512]{1,0:T(8,128)(2,1)}, bf16[1024,512]{1,0:T(8,128)(2,1)}, u32[]{:S(2)}, u32[]{:S(2)}) collective-permute-start(bf16[1024,512]{1,0:T(8,128)(2,1)} %param.6), channel_id=1, source_target_pairs={{0,1},{1,0},{2,3},{3,2},{4,5},{5,4},{6,7},{7,6},{8,9},{9,8},{10,11... | collective-permute-start | bytes 3145736 | tf_op jit(solution)/shard_map/ppermute | solution.py:201
  5.8 15.0 %collective-permute-start.12 = (bf16[512,512]{1,0:T(8,128)(2,1)S(1)}, bf16[512,512]{1,0:T(8,128)(2,1)}, u32[]{:S(2)}, u32[]{:S(2)}) collective-permute-start(bf16[512,512]{1,0:T(8,128)(2,1)S(1)} %get-tuple-element.7.near), channel_id=1, source_target_pairs={{2,0},{3,1},{0,2},{1,3},{6,4},{7,5},{4,6},{5,7},{10,8},{11,9},{8,1... | collective-permute-start | bytes 1572872 | tf_op jit(solution)/shard_map/ppermute | solution.py:201
  8.8 39.4 %slice-start = ((s8[14680064]{0:T(1024)(128)(4,1)}), s8[2097152]{0:T(1024)(128)(4,1)S(1)}, s32[]{:S(2)}) async-start(s8[14680064]{0:T(1024)(128)(4,1)} %bitcast.33), calls=%async_computation | async-start | bytes 4194304
  9.9 10.9 %collective-permute-start.16 = (bf16[512,512]{1,0:T(8,128)(2,1)S(1)}, bf16[512,512]{1,0:T(8,128)(2,1)}, u32[]{:S(2)}, u32[]{:S(2)}) collective-permute-start(bf16[512,512]{1,0:T(8,128)(2,1)S(1)} %get-tuple-element.7.near), channel_id=1, source_target_pairs={{4,2},{5,3},{2,4},{3,5},{12,10},{13,11},{10,12},{11,13},{20,18},{2... | collective-permute-start | bytes 1572872 | tf_op jit(solution)/shard_map/ppermute | solution.py:201
  11.4 20.5 %collective-permute-start = (bf16[512,512]{1,0:T(8,128)(2,1)S(1)}, bf16[512,512]{1,0:T(8,128)(2,1)}, u32[]{:S(2)}, u32[]{:S(2)}) collective-permute-start(bf16[512,512]{1,0:T(8,128)(2,1)S(1)} %get-tuple-element.8.near), channel_id=1, source_target_pairs={{2,0},{3,1},{0,2},{1,3},{6,4},{7,5},{4,6},{5,7},{10,8},{11,9},{8,1... | collective-permute-start | bytes 1572872 | tf_op jit(solution)/shard_map/ppermute | solution.py:201
  15.0 18.1 %collective-permute-start.4 = (bf16[512,512]{1,0:T(8,128)(2,1)S(1)}, bf16[512,512]{1,0:T(8,128)(2,1)}, u32[]{:S(2)}, u32[]{:S(2)}) collective-permute-start(bf16[512,512]{1,0:T(8,128)(2,1)S(1)} %get-tuple-element.8.near), channel_id=1, source_target_pairs={{4,2},{5,3},{2,4},{3,5},{12,10},{13,11},{10,12},{11,13},{20,18},{2... | collective-permute-start | bytes 1572872 | tf_op jit(solution)/shard_map/ppermute | solution.py:201
  20.8 39.4 %collective-permute-start.19 = (bf16[512,512]{1,0:T(8,128)(2,1)}, bf16[512,512]{1,0:T(8,128)(2,1)S(1)}, u32[]{:S(2)}, u32[]{:S(2)}) collective-permute-start(bf16[512,512]{1,0:T(8,128)(2,1)} %collective-permute-done.12.near), channel_id=1, source_target_pairs={{0,1},{1,0},{2,3},{3,2},{4,5},{5,4},{6,7},{7,6},{8,9},{9,8},{10,11... | collective-permute-start | bytes 1572872 | tf_op jit(solution)/shard_map/ppermute | solution.py:201
  20.8 39.9 %collective-permute-start.13 = (bf16[512,512]{1,0:T(8,128)(2,1)}, bf16[512,512]{1,0:T(8,128)(2,1)}, u32[]{:S(2)}, u32[]{:S(2)}) collective-permute-start(bf16[512,512]{1,0:T(8,128)(2,1)} %collective-permute-done.12.near), channel_id=1, source_target_pairs={{4,2},{5,3},{2,4},{3,5},{12,10},{13,11},{10,12},{11,13},{20,18},{2... | collective-permute-start | bytes 1572872 | tf_op jit(solution)/shard_map/ppermute | solution.py:201
  31.8 24.8 %collective-permute-start.17 = (bf16[512,512]{1,0:T(8,128)(2,1)}, bf16[512,512]{1,0:T(8,128)(2,1)S(1)}, u32[]{:S(2)}, u32[]{:S(2)}) collective-permute-start(bf16[512,512]{1,0:T(8,128)(2,1)} %collective-permute-done.16), channel_id=1, source_target_pairs={{2,0},{3,1},{4,6},{5,7},{10,8},{11,9},{12,14},{13,15},{18,16},{19,... | collective-permute-start | bytes 1572872 | tf_op jit(solution)/shard_map/ppermute | solution.py:201
  33.1 44.2 %collective-permute-start.7 = (bf16[512,512]{1,0:T(8,128)(2,1)}, bf16[512,512]{1,0:T(8,128)(2,1)S(1)}, u32[]{:S(2)}, u32[]{:S(2)}) collective-permute-start(bf16[512,512]{1,0:T(8,128)(2,1)} %collective-permute-done.near), channel_id=1, source_target_pairs={{0,1},{1,0},{2,3},{3,2},{4,5},{5,4},{6,7},{7,6},{8,9},{9,8},{10,11... | collective-permute-start | bytes 1572872 | tf_op jit(solution)/shard_map/ppermute | solution.py:201
  33.2 25.8 %collective-permute-start.5 = (bf16[512,512]{1,0:T(8,128)(2,1)}, bf16[512,512]{1,0:T(8,128)(2,1)}, u32[]{:S(2)}, u32[]{:S(2)}) collective-permute-start(bf16[512,512]{1,0:T(8,128)(2,1)} %collective-permute-done.4), channel_id=1, source_target_pairs={{2,0},{3,1},{4,6},{5,7},{10,8},{11,9},{12,14},{13,15},{18,16},{19,... | collective-permute-start | bytes 1572872 | tf_op jit(solution)/shard_map/ppermute | solution.py:201
  35.8 5.2 %copy-start = (bf16[4096,1792]{1,0:T(8,128)(2,1)S(1)}, bf16[4096,1792]{1,0:T(8,128)(2,1)}, u32[]{:S(2)}) copy-start(bf16[4096,1792]{1,0:T(8,128)(2,1)} %refs_1_.3) | copy-start | bytes 44040196
  41.0 7.3 %slice-start.1 = ((s8[14680064]{0:T(1024)(128)(4,1)}), s8[4194304]{0:T(1024)(128)(4,1)S(1)}, s32[]{:S(2)}) async-start(s8[14680064]{0:T(1024)(128)(4,1)} %bitcast.33), calls=%async_computation.1 | async-start | bytes 8388608
  41.0 7.3 %slice-start.2 = ((s8[14680064]{0:T(1024)(128)(4,1)}), s8[4194304]{0:T(1024)(128)(4,1)S(1)}, s32[]{:S(2)}) async-start(s8[14680064]{0:T(1024)(128)(4,1)} %bitcast.33), calls=%async_computation.2 | async-start | bytes 8388608
  41.0 7.3 %slice-start.3 = ((s8[14680064]{0:T(1024)(128)(4,1)}), s8[4194304]{0:T(1024)(128)(4,1)S(1)}, s32[]{:S(2)}) async-start(s8[14680064]{0:T(1024)(128)(4,1)} %bitcast.33), calls=%async_computation.3 | async-start | bytes 8388608
  48.2 8.4 %copy-start.1 = (f32[2,512,1792]{2,1,0:T(8,128)}, f32[2,512,1792]{2,1,0:T(8,128)S(1)}, u32[]{:S(2)}) copy-start(f32[2,512,1792]{2,1,0:T(8,128)S(1)} %shard_map.67.before) | copy-start | bytes 22020100
  56.7 5.3 %collective-permute-start.1 = (bf16[512,512]{1,0:T(8,128)(2,1)}, bf16[512,512]{1,0:T(8,128)(2,1)S(1)}, u32[]{:S(2)}, u32[]{:S(2)}) collective-permute-start(bf16[512,512]{1,0:T(8,128)(2,1)} %collective-permute-done.near), channel_id=1, source_target_pairs={{4,2},{5,3},{2,4},{3,5},{12,10},{13,11},{10,12},{11,13},{20,18},{2... | collective-permute-start | bytes 1572872 | tf_op jit(solution)/shard_map/ppermute | solution.py:201
  59.0 36.3 %collective-permute-start.18 = (bf16[512,512]{1,0:T(8,128)(2,1)S(1)}, bf16[512,512]{1,0:T(8,128)(2,1)S(1)}, u32[]{:S(2)}, u32[]{:S(2)}) collective-permute-start(bf16[512,512]{1,0:T(8,128)(2,1)S(1)} %broadcast_select_fusion.near), channel_id=1, source_target_pairs={{0,1},{1,0},{2,3},{3,2},{4,5},{5,4},{6,7},{7,6},{8,9},{9,8},{10,11... | collective-permute-start | bytes 1572872 | tf_op jit(solution)/shard_map/ppermute | solution.py:201
  60.1 48.5 %collective-permute-start.6 = (bf16[512,512]{1,0:T(8,128)(2,1)S(1)}, bf16[512,512]{1,0:T(8,128)(2,1)S(1)}, u32[]{:S(2)}, u32[]{:S(2)}) collective-permute-start(bf16[512,512]{1,0:T(8,128)(2,1)S(1)} %broadcast_select_fusion.1.near), channel_id=1, source_target_pairs={{0,1},{1,0},{2,3},{3,2},{4,5},{5,4},{6,7},{7,6},{8,9},{9,8},{10,11... | collective-permute-start | bytes 1572872 | tf_op jit(solution)/shard_map/ppermute | solution.py:201
  60.7 24.5 %collective-permute-start.14 = (bf16[512,512]{1,0:T(8,128)(2,1)}, bf16[512,512]{1,0:T(8,128)(2,1)S(1)}, u32[]{:S(2)}, u32[]{:S(2)}) collective-permute-start(bf16[512,512]{1,0:T(8,128)(2,1)} %collective-permute-done.13), channel_id=1, source_target_pairs={{2,0},{3,1},{4,6},{5,7},{10,8},{11,9},{12,14},{13,15},{18,16},{19,... | collective-permute-start | bytes 1572872 | tf_op jit(solution)/shard_map/ppermute | solution.py:201
  62.0 33.1 %collective-permute-start.2 = (bf16[512,512]{1,0:T(8,128)(2,1)S(1)}, bf16[512,512]{1,0:T(8,128)(2,1)S(1)}, u32[]{:S(2)}, u32[]{:S(2)}) collective-permute-start(bf16[512,512]{1,0:T(8,128)(2,1)S(1)} %collective-permute-done.1), channel_id=1, source_target_pairs={{2,0},{3,1},{4,6},{5,7},{10,8},{11,9},{12,14},{13,15},{18,16},{19,... | collective-permute-start | bytes 1572872 | tf_op jit(solution)/shard_map/ppermute | solution.py:201
  63.5 3.1 %copy-start.2 = (f32[2,512,1792]{2,1,0:T(8,128)S(1)}, f32[2,512,1792]{2,1,0:T(8,128)}, u32[]{:S(2)}) copy-start(f32[2,512,1792]{2,1,0:T(8,128)} %copy-done.1) | copy-start | bytes 22020100
  74.4 2.9 %copy-start.3 = (f32[2,512,1792]{2,1,0:T(8,128)}, f32[2,512,1792]{2,1,0:T(8,128)S(1)}, u32[]{:S(2)}) copy-start(f32[2,512,1792]{2,1,0:T(8,128)S(1)} %shard_map.68.before) | copy-start | bytes 22020100
  85.3 31.0 %collective-permute-start.15 = (bf16[512,512]{1,0:T(8,128)(2,1)S(1)}, bf16[512,512]{1,0:T(8,128)(2,1)S(1)}, u32[]{:S(2)}, u32[]{:S(2)}) collective-permute-start(bf16[512,512]{1,0:T(8,128)(2,1)S(1)} %broadcast_select_fusion.2.near), channel_id=1, source_target_pairs={{0,1},{1,0},{2,3},{3,2},{4,5},{5,4},{6,7},{7,6},{8,9},{9,8},{10,11... | collective-permute-start | bytes 1572872 | tf_op jit(solution)/shard_map/ppermute | solution.py:201
  95.2 30.0 %collective-permute-start.3 = (bf16[512,512]{1,0:T(8,128)(2,1)S(1)}, bf16[512,512]{1,0:T(8,128)(2,1)S(1)}, u32[]{:S(2)}, u32[]{:S(2)}) collective-permute-start(bf16[512,512]{1,0:T(8,128)(2,1)S(1)} %broadcast_select_fusion.3.near), channel_id=1, source_target_pairs={{0,1},{1,0},{2,3},{3,2},{4,5},{5,4},{6,7},{7,6},{8,9},{9,8},{10,11... | collective-permute-start | bytes 1572872 | tf_op jit(solution)/shard_map/ppermute | solution.py:201
  95.3 3.1 %copy-start.4 = (f32[2,512,1792]{2,1,0:T(8,128)S(1)}, f32[2,512,1792]{2,1,0:T(8,128)}, u32[]{:S(2)}) copy-start(f32[2,512,1792]{2,1,0:T(8,128)} %copy-done.3) | copy-start | bytes 22020100
  105.7 2.9 %copy-start.5 = (f32[2,512,1792]{2,1,0:T(8,128)}, f32[2,512,1792]{2,1,0:T(8,128)S(1)}, u32[]{:S(2)}) copy-start(f32[2,512,1792]{2,1,0:T(8,128)S(1)} %shard_map.69.before) | copy-start | bytes 22020100
  108.6 7.7 %copy-start.7 = (f32[512,1]{1,0:T(8,128)S(1)}, f32[512,1]{1,0:T(8,128)}, u32[]{:S(2)}) copy-start(f32[512,1]{1,0:T(8,128)} %copy.12.factor) | copy-start | bytes 6148
  108.6 7.7 %copy-start.6 = (f32[2,512,1792]{2,1,0:T(8,128)S(1)}, f32[2,512,1792]{2,1,0:T(8,128)}, u32[]{:S(2)}) copy-start(f32[2,512,1792]{2,1,0:T(8,128)} %copy-done.5) | copy-start | bytes 22020100
  134.6 9.2 %collective-permute-start.20 = (bf16[448,256]{0,1:T(8,128)(2,1)S(1)}, bf16[448,256]{0,1:T(8,128)(2,1)S(1)}, u32[]{:S(2)}, u32[]{:S(2)}) collective-permute-start(bf16[448,256]{0,1:T(8,128)(2,1)S(1)} %get-tuple-element.9), channel_id=1, source_target_pairs={{0,8},{8,0},{16,24},{24,16},{1,9},{9,1},{17,25},{25,17},{2,10},{10... | collective-permute-start | bytes 688136 | tf_op jit(solution)/shard_map/ppermute | solution.py:181
  136.1 14.0 %collective-permute-start.21 = (bf16[448,256]{0,1:T(8,128)(2,1)S(1)}, bf16[448,256]{0,1:T(8,128)(2,1)S(1)}, u32[]{:S(2)}, u32[]{:S(2)}) collective-permute-start(bf16[448,256]{0,1:T(8,128)(2,1)S(1)} %get-tuple-element.11), channel_id=1, source_target_pairs={{0,16},{8,24},{16,0},{24,8},{1,17},{9,25},{17,1},{25,9},{2,18},{10... | collective-permute-start | bytes 688136 | tf_op jit(solution)/shard_map/ppermute | solution.py:181
  137.7 12.5 %collective-permute-start.22 = (bf16[448,256]{0,1:T(8,128)(2,1)S(1)}, bf16[448,256]{0,1:T(8,128)(2,1)S(1)}, u32[]{:S(2)}, u32[]{:S(2)}) collective-permute-start(bf16[448,256]{0,1:T(8,128)(2,1)S(1)} %get-tuple-element.10), channel_id=1, source_target_pairs={{0,24},{8,16},{16,8},{24,0},{1,25},{9,17},{17,9},{25,1},{2,26},{10... | collective-permute-start | bytes 688136 | tf_op jit(solution)/shard_map/ppermute | solution.py:181
  150.7 4.3 %collective-permute-start.23 = (f32[64,256]{1,0:T(8,128)S(1)}, f32[64,256]{1,0:T(8,128)S(1)}, u32[]{:S(2)}, u32[]{:S(2)}) collective-permute-start(f32[64,256]{1,0:T(8,128)S(1)} %get-tuple-element.14), channel_id=1, source_target_pairs={{0,8},{8,0},{16,24},{24,16},{1,9},{9,1},{17,25},{25,17},{2,10},{10... | collective-permute-start | bytes 196616 | tf_op jit(solution)/shard_map/ppermute | solution.py:181
  152.0 4.6 %collective-permute-start.24 = (f32[64,256]{1,0:T(8,128)S(1)}, f32[64,256]{1,0:T(8,128)S(1)}, u32[]{:S(2)}, u32[]{:S(2)}) collective-permute-start(f32[64,256]{1,0:T(8,128)S(1)} %get-tuple-element.16), channel_id=1, source_target_pairs={{0,16},{8,24},{16,0},{24,8},{1,17},{9,25},{17,1},{25,9},{2,18},{10... | collective-permute-start | bytes 196616 | tf_op jit(solution)/shard_map/ppermute | solution.py:181
  152.8 5.2 %collective-permute-start.25 = (f32[64,256]{1,0:T(8,128)S(1)}, f32[64,256]{1,0:T(8,128)S(1)}, u32[]{:S(2)}, u32[]{:S(2)}) collective-permute-start(f32[64,256]{1,0:T(8,128)S(1)} %get-tuple-element.15), channel_id=1, source_target_pairs={{0,24},{8,16},{16,8},{24,0},{1,25},{9,17},{17,9},{25,1},{2,26},{10... | collective-permute-start | bytes 196616 | tf_op jit(solution)/shard_map/ppermute | solution.py:181
  158.0 12.0 %collective-permute-start.26 = (f32[64,256]{1,0:T(8,128)S(1)}, f32[64,256]{1,0:T(8,128)S(1)}, u32[]{:S(2)}, u32[]{:S(2)}) collective-permute-start(f32[64,256]{1,0:T(8,128)S(1)} %add_add_fusion.1), channel_id=1, source_target_pairs={{0,2},{1,3},{2,0},{3,1},{4,6},{5,7},{6,4},{7,5},{8,10},{9,11},{10,... | collective-permute-start | bytes 196616 | tf_op jit(solution)/shard_map/ppermute | solution.py:201
  167.4 5.9 %collective-permute-start.27 = (f32[64,256]{1,0:T(8,128)S(1)}, f32[64,256]{1,0:T(8,128)S(1)}, u32[]{:S(2)}, u32[]{:S(2)}) collective-permute-start(f32[64,256]{1,0:T(8,128)S(1)} %add_add_fusion.1), channel_id=1, source_target_pairs={{0,4},{1,5},{2,6},{3,7},{4,0},{5,1},{6,2},{7,3},{8,12},{9,13},{10,... | collective-permute-start | bytes 196616 | tf_op jit(solution)/shard_map/ppermute | solution.py:201
  168.6 6.2 %collective-permute-start.28 = (f32[64,256]{1,0:T(8,128)S(1)}, f32[64,256]{1,0:T(8,128)S(1)}, u32[]{:S(2)}, u32[]{:S(2)}) collective-permute-start(f32[64,256]{1,0:T(8,128)S(1)} %add_add_fusion.1), channel_id=1, source_target_pairs={{0,6},{1,7},{2,4},{3,5},{4,2},{5,3},{6,0},{7,1},{8,14},{9,15},{10,... | collective-permute-start | bytes 196616 | tf_op jit(solution)/shard_map/ppermute | solution.py:201
  174.8 1.3 collective-permute-start.29
